TPU v7x, 32 devices: a whole 2x2x4 slice. The times are simulated.
32 devices in a mesh: wshard: 8 (over z, x), seq: 4 (over y, core).
Axes of the slice: x: 2, y: 2, z: 4, core: 2. Of those that a mesh axis runs over, the one named last changes fastest.
Arguments:
- hidden: bfloat16 [8, 2048, 1536], P('wshard', 'seq'), may hold values from -6 to 6
- segments: int32 [8, 2048], P('wshard'), may hold values from 0 to 3, never falling along the last dimension, each value on 1 to 1024 neighbouring positions
- norm_gain: bfloat16 [1536], P('wshard'), may hold values from 0.099609375 to 1.8984375
- in_weight: bfloat16 [1536, 6448], P('wshard'), may hold values from -0.15625 to 0.15625
- conv_weight: float32 [4, 3328], replicated, may hold values from -3 to 3
- conv_bias: float32 [3328], replicated, may hold values from -3 to 3
- step_bias: float32 [48], replicated, may hold values from -6 to -2
- decay_log: float32 [48], replicated, may hold values from 0 to 2.5
- skip_scale: float32 [48], replicated, may hold values from 0.5 to 1.5
- gate_gain: bfloat16 [3072], P('wshard'), may hold values from 0.099609375 to 1.8984375
- out_weight: bfloat16 [3072, 1536], P('wshard'), may hold values from -0.109375 to 0.109375
- cotangent: bfloat16 [8, 2048, 1536], P('wshard', 'seq'), may hold values from -6 to 6
Outputs:
- layer_output: float32 [8, 2048, 1536], P('wshard', 'seq')
- hidden_grad: float32 [8, 2048, 1536], P('wshard', 'seq')
- norm_gain_grad: float32 [1536], P('wshard')
- in_weight_grad: float32 [1536, 6448], P('wshard')
- conv_weight_grad: float32 [4, 3328], replicated
- conv_bias_grad: float32 [3328], replicated
- step_bias_grad: float32 [48], replicated
- decay_log_grad: float32 [48], replicated
- skip_scale_grad: float32 [48], replicated
- gate_gain_grad: float32 [3072], P('wshard')
- out_weight_grad: float32 [3072, 1536], P('wshard')
Inputs may be any that keep to these rules, and one draw needn't show every extreme that they name: `segments`: within each sequence document numbers never fall; each document spans 1 to 1024 consecutive tokens, one of them exactly that many.
All inputs are finite; a program needn't handle non-finite values.
Results may differ from a plain program's by a relative error of at most 0.011.
Values may be sent and summed in bfloat16 or wider, within the bound.
A program may use at most 256 MiB of HBM per device.

v0:
```python
import jax
import jax.numpy as jnp
from jax import lax
from jax.sharding import PartitionSpec as P

D = 1536
H = 48
P_SIZE = 64
N = 128
STRETCH = 256
E = 3072
eps = 1e-05
precise = lax.Precision.HIGHEST


def causal_conv(values, kernel, offsets, seg_ids):
    tap_count = kernel.shape[0]
    length_here = values.shape[0]
    padded = jnp.pad(values, ((tap_count - 1, 0), (0, 0)))
    seg_padded = jnp.concatenate([jnp.full((tap_count - 1,), -1, jnp.int32), seg_ids])
    summed = jnp.zeros_like(values) + offsets[None, :]
    for offset in range(tap_count):
        same_doc = (seg_padded[offset : offset + length_here] == seg_ids).astype(values.dtype)
        summed = (
            summed
            + kernel[offset][None, :] * padded[offset : offset + length_here] * same_doc[:, None]
        )
    return jax.nn.silu(summed)


def block_step(state, pieces):
    x_block, b_block, c_block, rate_block, step_block, seg_block, seg_before = pieces
    block_len = x_block.shape[0]
    cumul = jnp.cumsum(rate_block, axis=0)
    causal = jnp.arange(block_len)[:, None] >= jnp.arange(block_len)[None, :]
    allowed = (causal & (seg_block[:, None] == seg_block[None, :]))[:, :, None]
    spread = cumul[:, None, :] - cumul[None, :, :]
    decay = jnp.where(allowed, jnp.exp(jnp.where(allowed, spread, 0.0)), 0.0)
    affinity = jnp.dot(c_block, b_block.T, precision=precise)
    weighted = affinity[:, :, None] * decay * step_block[None, :, :]
    within = jnp.einsum("ijh,jhp->ihp", weighted, x_block, precision=precise)
    carried = (seg_block == seg_before).astype(rate_block.dtype)
    entering = (
        jnp.einsum("in,hnp->ihp", c_block, state, precision=precise)
        * (jnp.exp(cumul) * carried[:, None])[:, :, None]
    )
    last_cum = cumul[block_len - 1]
    same_last = (seg_block == seg_block[block_len - 1]).astype(rate_block.dtype)
    to_end = jnp.exp(last_cum[None, :] - cumul) * same_last[:, None] * step_block
    retained = jnp.exp(last_cum) * (seg_block[block_len - 1] == seg_before).astype(rate_block.dtype)
    new_state = state * retained[:, None, None] + jnp.einsum(
        "jn,jh,jhp->hnp", b_block, to_end, x_block, precision=precise
    )
    return (new_state, within + entering)


def state_scan(x_heads, b_vals, c_vals, decay_rates, step_sizes, seg_ids):
    length_here, head_count, head_dim = x_heads.shape
    blocks = length_here // STRETCH
    seg_blocks = seg_ids.reshape(blocks, STRETCH)
    seg_prior = jnp.concatenate([jnp.full((1,), -1, jnp.int32), seg_blocks[:-1, STRETCH - 1]])
    start_state = jnp.zeros((head_count, b_vals.shape[1], head_dim), x_heads.dtype)
    pieces = (
        x_heads.reshape(blocks, STRETCH, head_count, head_dim),
        b_vals.reshape(blocks, STRETCH, b_vals.shape[1]),
        c_vals.reshape(blocks, STRETCH, c_vals.shape[1]),
        decay_rates.reshape(blocks, STRETCH, head_count),
        step_sizes.reshape(blocks, STRETCH, head_count),
        seg_blocks,
        seg_prior,
    )
    _, results = lax.scan(jax.checkpoint(block_step), start_state, pieces)
    return results.reshape(length_here, head_count, head_dim)


def mixer(
    x_raw,
    bc_raw,
    dt_raw,
    conv_weight,
    conv_bias,
    step_bias,
    decay_log,
    skip_scale,
    seg_ids,
    head_start,
    chan_start,
):
    channels = x_raw.shape[1]
    head_count = dt_raw.shape[1]
    head_dim = channels // head_count
    state_dim = bc_raw.shape[1] // 2
    inner_width = conv_weight.shape[1] - 2 * state_dim
    x_conv = causal_conv(
        x_raw,
        lax.dynamic_slice_in_dim(conv_weight, chan_start, channels, 1),
        lax.dynamic_slice_in_dim(conv_bias, chan_start, channels, 0),
        seg_ids,
    )
    bc_conv = causal_conv(bc_raw, conv_weight[:, inner_width:], conv_bias[inner_width:], seg_ids)
    x_heads = x_conv.reshape(-1, head_count, head_dim)
    step_sizes = jax.nn.softplus(
        dt_raw + lax.dynamic_slice_in_dim(step_bias, head_start, head_count, 0)[None, :]
    )
    decay_rates = -jnp.exp(lax.dynamic_slice_in_dim(decay_log, head_start, head_count, 0))
    scanned = state_scan(
        x_heads,
        bc_conv[:, :state_dim],
        bc_conv[:, state_dim:],
        step_sizes * decay_rates[None, :],
        step_sizes,
        seg_ids,
    )
    skipped = (
        scanned
        + lax.dynamic_slice_in_dim(skip_scale, head_start, head_count, 0)[None, :, None] * x_heads
    )
    return skipped.reshape(-1, channels)


def pre_norm(hidden_rows, gain_full):
    scale = lax.rsqrt(jnp.mean(hidden_rows * hidden_rows, axis=-1, keepdims=True) + eps)
    return hidden_rows * scale * gain_full[None, :]


def gated_norm(mixed_rows, gate_part, gain_full):
    gated = mixed_rows * jax.nn.silu(gate_part)
    gate_scale = lax.rsqrt(jnp.mean(gated * gated, axis=-1, keepdims=True) + eps)
    return gated * gate_scale * gain_full[None, :]


def over_rows(left, right):
    return lax.dot_general(
        left, right, (((0,), (0,)), ((), ())), preferred_element_type=jnp.float32
    )


def shards(
    hidden,
    segments,
    norm_gain,
    in_weight,
    conv_weight,
    conv_bias,
    step_bias,
    decay_log,
    skip_scale,
    gate_gain,
    out_weight,
    cotangent,
):
    seq_count, piece_len, _ = hidden.shape
    row_count = seq_count * piece_len
    group_heads = H // lax.axis_size("seq")
    head_start = lax.axis_index("seq") * group_heads
    chan_start = head_start * P_SIZE
    in_full, norm_full, out_full, gate_full = (
        lax.all_gather(in_weight, "wshard", axis=0, tiled=True),
        lax.all_gather(norm_gain, "wshard", axis=0, tiled=True),
        lax.all_gather(out_weight, "wshard", axis=0, tiled=True),
        lax.all_gather(gate_gain, "wshard", axis=0, tiled=True),
    )
    hidden_rows = hidden.astype(jnp.float32).reshape(row_count, D)
    normed_low = pre_norm(hidden_rows, norm_full.astype(jnp.float32)).astype(jnp.bfloat16)
    projected = jnp.dot(normed_low, in_full, preferred_element_type=jnp.float32)
    gate_part = projected[:, :E]
    x_low = projected[:, E : 2 * E].astype(jnp.bfloat16).reshape(seq_count, piece_len, E)
    bc_low = (
        projected[:, 2 * E : 2 * E + 2 * N]
        .astype(jnp.bfloat16)
        .reshape(seq_count, piece_len, 2 * N)
    )
    dt_low = projected[:, 2 * E + 2 * N :].astype(jnp.bfloat16).reshape(seq_count, piece_len, H)
    x_heads, dt_heads = (
        lax.all_to_all(x_low, "seq", split_axis=2, concat_axis=1, tiled=True),
        lax.all_to_all(dt_low, "seq", split_axis=2, concat_axis=1, tiled=True),
    )
    bc_whole = lax.all_gather(bc_low, "seq", axis=1, tiled=True)

    def mixer_all(x_in, bc_in, dt_in, kernel, offsets, bias_in, log_in, skip_in):

        def one_seq(items):
            x_seq, bc_seq, dt_seq, seg_seq = items
            return mixer(
                x_seq,
                bc_seq,
                dt_seq,
                kernel,
                offsets,
                bias_in,
                log_in,
                skip_in,
                seg_seq,
                head_start,
                chan_start,
            )

        return lax.map(one_seq, (x_in, bc_in, dt_in, segments))

    mixed_heads, mixer_pull = jax.vjp(
        mixer_all,
        x_heads.astype(jnp.float32),
        bc_whole.astype(jnp.float32),
        dt_heads.astype(jnp.float32),
        conv_weight,
        conv_bias,
        step_bias,
        decay_log,
        skip_scale,
    )
    mixed_pieces = lax.all_to_all(
        mixed_heads.astype(jnp.bfloat16), "seq", split_axis=1, concat_axis=2, tiled=True
    )
    mixed_rows = mixed_pieces.reshape(row_count, E).astype(jnp.float32)
    gated_low = gated_norm(mixed_rows, gate_part, gate_full.astype(jnp.float32)).astype(
        jnp.bfloat16
    )
    layer_output = hidden_rows + jnp.dot(gated_low, out_full, preferred_element_type=jnp.float32)
    cot_rows = cotangent.reshape(row_count, D)
    d_gated = lax.dot_general(
        cot_rows, out_full, (((1,), (1,)), ((), ())), preferred_element_type=jnp.float32
    )
    _, gate_pull = jax.vjp(gated_norm, mixed_rows, gate_part, gate_full.astype(jnp.float32))
    d_mixed, d_gate_part, gate_gain_term = gate_pull(d_gated)
    d_mixed_heads = lax.all_to_all(
        d_mixed.astype(jnp.bfloat16).reshape(seq_count, piece_len, E),
        "seq",
        split_axis=2,
        concat_axis=1,
        tiled=True,
    )
    d_x_heads, d_bc_whole, d_dt_heads, kernel_sum, offset_sum, bias_sum, log_sum, skip_sum = (
        mixer_pull(d_mixed_heads.astype(jnp.float32))
    )
    conv_weight_grad, conv_bias_grad, step_bias_grad, decay_log_grad, skip_scale_grad = lax.psum(
        (kernel_sum, offset_sum, bias_sum, log_sum, skip_sum), ("wshard", "seq")
    )
    d_x_low = d_x_heads.astype(jnp.bfloat16)
    d_dt_low = d_dt_heads.astype(jnp.bfloat16)
    d_x_pieces, d_dt_pieces = (
        lax.all_to_all(d_x_low, "seq", split_axis=1, concat_axis=2, tiled=True),
        lax.all_to_all(d_dt_low, "seq", split_axis=1, concat_axis=2, tiled=True),
    )
    d_bc_pieces = lax.psum_scatter(
        d_bc_whole.astype(jnp.bfloat16), "seq", scatter_dimension=1, tiled=True
    )
    d_gate_low = d_gate_part.astype(jnp.bfloat16)
    d_projected = jnp.concatenate(
        [
            d_gate_low,
            d_x_pieces.reshape(row_count, E),
            d_bc_pieces.reshape(row_count, 2 * N),
            d_dt_pieces.reshape(row_count, H),
        ],
        axis=1,
    )
    d_normed = lax.dot_general(
        d_projected, in_full, (((1,), (1,)), ((), ())), preferred_element_type=jnp.float32
    )
    _, norm_pull = jax.vjp(pre_norm, hidden_rows, norm_full.astype(jnp.float32))
    hidden_term, norm_gain_term = norm_pull(d_normed)
    hidden_grad = (cot_rows.astype(jnp.float32) + hidden_term).reshape(seq_count, piece_len, D)
    in_weight_term = over_rows(normed_low, d_projected)
    out_weight_term = over_rows(gated_low, cot_rows)
    shard_sums = (
        lax.psum_scatter(in_weight_term, "wshard", scatter_dimension=0, tiled=True),
        lax.psum_scatter(norm_gain_term, "wshard", scatter_dimension=0, tiled=True),
        lax.psum_scatter(out_weight_term, "wshard", scatter_dimension=0, tiled=True),
        lax.psum_scatter(gate_gain_term, "wshard", scatter_dimension=0, tiled=True),
    )
    in_weight_grad, norm_gain_grad, out_weight_grad, gate_gain_grad = (
        lax.psum(shard_sums[0].astype(jnp.bfloat16), "seq").astype(jnp.float32),
        lax.psum(shard_sums[1].astype(jnp.bfloat16), "seq").astype(jnp.float32),
        lax.psum(shard_sums[2].astype(jnp.bfloat16), "seq").astype(jnp.float32),
        lax.psum(shard_sums[3].astype(jnp.bfloat16), "seq").astype(jnp.float32),
    )
    return (
        layer_output.reshape(seq_count, piece_len, D),
        hidden_grad,
        norm_gain_grad,
        in_weight_grad,
        conv_weight_grad,
        conv_bias_grad,
        step_bias_grad,
        decay_log_grad,
        skip_scale_grad,
        gate_gain_grad,
        out_weight_grad,
    )


def solution(mesh):
    in_specs = (
        P("wshard", "seq", None),
        P("wshard", None),
        P("wshard"),
        P("wshard", None),
        P(),
        P(),
        P(),
        P(),
        P(),
        P("wshard"),
        P("wshard", None),
        P("wshard", "seq", None),
    )
    out_specs = (
        P("wshard", "seq", None),
        P("wshard", "seq", None),
        P("wshard"),
        P("wshard", None),
        P(),
        P(),
        P(),
        P(),
        P(),
        P("wshard"),
        P("wshard", None),
    )
    return jax.shard_map(shards, mesh=mesh, in_specs=in_specs, out_specs=out_specs, check_vma=False)
```

profile of v0, /device:TPU:8, one launch (start us, length us, event | category | flops | bytes accessed | tf_op | source)
XLA Modules:
  0.0 2988.3 jit_solution(9371011800629736709)
XLA Ops:
  10.8 43.2 %all-reduce.24 = bf16[1536]{0:T(1024)(128)(2,1)S(1)} all-reduce(bf16[1536]{0:T(1024)(128)(2,1)S(1)} %dynamic-update-slice.15), channel_id=1, replica_groups=mesh['wshard'=8,'seq'=4] {'wshard'}, use_global_device_ids=true, to_apply=%add.24 | all-reduce | flops 1536 | bytes 6144
  56.5 339.2 %all-gather.6.cloned.1.call-done = bf16[1536,6448]{1,0:T(8,128)(2,1)} async-done(((bf16[192,6448]{1,0:T(8,128)(2,1)}), bf16[1536,6448]{1,0:T(8,128)(2,1)}) %all-gather.6.cloned.1.call-update) | async-done | bytes 19808272 | tf_op jit(solution)/shard_map/all_gather | solution.py:158
  425.8 27.4 copy.490
  453.2 20.3 reduce.35
  575.2 312.3 %while.143 = (s32[]{:T(128)}, f32[12,128,64]{1,2,0:T(8,128)S(1)}, f32[8,256,12,64]{1,0,3,2:T(8,128)}, f32[8,12,128,64]{2,3,1,0:T(8,128)}, f32[8,256,12]{1,2,0:T(...) while((s32[]{:T(128)}, f32[12,128,64]{1,2,0:T(8,128)S(1)}, ...), condition=%wide.region_4.5_spmd.clone, body=%wide.region_1.4_spmd.clone.sunk | while | flops 1314042880 | bytes 11014881 | solution.py:72
  592.4 18.5 dynamic_update_slice.219
  631.4 18.5 dynamic_update_slice.219
  670.4 18.5 dynamic_update_slice.219
  709.4 18.5 dynamic_update_slice.219
  748.4 18.5 dynamic_update_slice.219
  787.5 18.5 dynamic_update_slice.219
  826.5 18.5 dynamic_update_slice.219
  865.5 18.5 dynamic_update_slice.219
  908.2 44.7 %copy.489 = bf16[1,2048,768]{2,0,1:T(2,128)(2,1)} copy(bf16[1,2048,768]{2,1,0:T(8,128)(2,1)S(1)} %fusion.107) | data formatting | bytes 6291456 | tf_op jit(solution)/shard_map/convert_element_type | solution.py:212
  952.9 31.6 %reduce.36 = bf16[2048,768]{1,0:T(8,128)(2,1)S(1)} reduce(bf16[2048,1,768]{2,1,0:T(2,128)(2,1)} %bitcast.482, bf16[]{:T(256)} %broadcast.726), dimensions={1}, to_apply=%bitcast.320.reduce_sub_computation | reduce | bytes 6291458
  990.7 24.7 all-gather.1
  1073.3 27.4 copy.488
  1100.7 20.4 reduce.37
  1128.4 36.8 %all-to-all-done.3 = bf16[4,2,196608]{2,1,0:T(2,128)(2,1)S(1)} async-done(((bf16[4,2,196608]{2,1,0:T(2,128)(2,1)}), bf16[4,2,196608]{2,1,0:T(2,128)(2,1)S(1)}, u32[]{:S(2)}, u32[]{:S(2)}) %all-to-all-start.3) | async-done | bytes 3145760 | tf_op jit(solution)/shard_map/all_to_all | solution.py:225
  1198.6 566.3 %while.144 = (s32[]{:T(128)}, f32[12,128,64]{1,2,0:T(8,128)S(1)}, f32[8,256,12,64]{1,0,3,2:T(8,128)}, f32[8,256,128]{2,1,0:T(8,128)}, f32[8,256,128]{2,1,0:T(8,1...) while((s32[]{:T(128)}, f32[12,128,64]{1,2,0:T(8,128)S(1)}, ...), condition=%wide.region_19.20_spmd.clone, body=%wide.region_7.19_spmd.clone.sunk | while | flops 3038930944 | bytes 28993192 | solution.py:72
  1245.8 18.5 dynamic_update_slice.223
  1599.3 18.5 dynamic_update_slice.223
  1831.3 20.7 multiply_reduce_fusion.7
  1863.9 44.8 %copy.487 = bf16[1,2048,768]{2,0,1:T(2,128)(2,1)} copy(bf16[1,2048,768]{2,1,0:T(8,128)(2,1)S(1)} %fusion.111) | data formatting | bytes 6291456 | tf_op jit(solution)/shard_map/convert_element_type | solution.py:238
  1908.6 31.6 %reduce.39 = bf16[2048,768]{1,0:T(8,128)(2,1)S(1)} reduce(bf16[2048,1,768]{2,1,0:T(2,128)(2,1)} %bitcast.476, bf16[]{:T(256)} %broadcast.726), dimensions={1}, to_apply=%bitcast.318.reduce_sub_computation | reduce | bytes 6291458
  1951.7 31.7 %all-to-all-done.4 = bf16[4,2,196608]{2,1,0:T(2,128)(2,1)S(1)} async-done(((bf16[4,2,196608]{2,1,0:T(2,128)(2,1)}), bf16[4,2,196608]{2,1,0:T(2,128)(2,1)S(1)}, u32[]{:S(2)}, u32[]{:S(2)}) %all-to-all-start.4) | async-done | bytes 3145760 | tf_op jit(solution)/shard_map/all_to_all | solution.py:241
  1997.5 20.9 fusion.120
  2019.8 99.0 %reduce-scatter.8.cloned.1.call-done = f32[384,1536]{1,0:T(8,128)} async-done(((f32[3072,1536]{1,0:T(8,128)}), f32[384,1536]{1,0:T(8,128)}) %reduce-scatter.8.cloned.1.call-update) | async-done | bytes 2359312 | tf_op jit(solution)/shard_map/reduce_scatter | solution.py:268
  2121.6 640.6 %reduce-scatter.6.cloned.1.call-done = f32[192,6448]{1,0:T(8,128)} async-done(((f32[1536,6448]{1,0:T(8,128)}), f32[192,6448]{1,0:T(8,128)}) %reduce-scatter.6.cloned.1.call-update) | async-done | bytes 4952080 | tf_op jit(solution)/shard_map/reduce_scatter | solution.py:266
  2780.2 26.7 fusion.104
  2811.4 33.8 %all-reduce.28 = (bf16[1536]{0:T(1024)(128)(2,1)S(1)}, bf16[3072]{0:T(1024)(128)(2,1)S(1)}) all-reduce(f32[1536]{0:T(1024)S(1)} %get-tuple-element.1746, f32[3072]{0:T(1024)S(1)} %copy-done.45), channel_id=4, replica_groups=mesh['wshard'=8,'seq'=4] {'wshard'}, use_global_device_ids=true, to_apply=%region_23.24.clone | all-reduce | flops 4608 | bytes 27648
  2858.2 117.0 %all-reduce.34.cloned.1.call-done = (f32[4,3328]{1,0:T(4,128)}, f32[3328]{0:T(1024)}, f32[48]{0:T(128)}, f32[48]{0:T(128)}, f32[48]{0:T(128)}) async-done(((f32[4,3328]{1,0:T(4,128)}, f32[3328]{0:T(1024)}, f32[48]{0:T(128)}, f32[48]{0:T(128)}, f32[48]{0:T(128)}), (f32[4,3328]{1,0:T(4,128)}, f32[3328]{0:T(1024)}, f32[48]{0:T(128)}, f32[48]{0:T(128)}, f32[48]{0:T(128)})) %all-reduce.34.cloned.1.call-update) | async-done | bytes 67152 | tf_op jit(solution)/shard_map/psum | solution.py:235
  (1040 shorter events, 1080.1 us)
Async XLA Ops:
  7.2 388.5 %all-gather.6.cloned.1.call-start = ((), (), s32[]{:S(2)}) async-start(), calls=%async_computation.9 | async-start | bytes 22560768 | tf_op jit(solution)/shard_map/all_gather | solution.py:158
  7.9 494.1 %all-gather.10.cloned.1.call-start = ((), (), s32[]{:S(2)}) async-start(), calls=%async_computation.14 | async-start | bytes 1310720 | tf_op jit(solution)/shard_map/all_gather | solution.py:178
  54.0 359.0 %copy-start.39 = (f32[1536]{0:T(1024)}, f32[1536]{0:T(1024)S(1)}, u32[]{:S(2)}) copy-start(f32[1536]{0:T(1024)S(1)} %convert_element_type.262) | copy-start | bytes 18436
  56.5 356.6 %copy-start.50 = (f32[512]{0:T(512)}, f32[512]{0:T(512)S(1)}, u32[]{:S(2)}) copy-start(f32[512]{0:T(512)S(1)} %fusion.144) | copy-start | bytes 6148
  416.5 636.6 %all-gather.8.cloned.1.call-start = ((), (), s32[]{:S(2)}) async-start(), calls=%async_computation.10 | async-start | bytes 10616832 | tf_op jit(solution)/shard_map/all_gather | solution.py:160
  420.2 56.9 %all-to-all-start = ((bf16[4,2,3072]{2,1,0:T(2,128)(2,1)}), bf16[4,2,3072]{2,1,0:T(2,128)(2,1)S(1)}, u32[]{:S(2)}, u32[]{:S(2)}) async-start(bf16[4,2,3072]{2,1,0:T(2,128)(2,1)} %reshape.1078), calls=%async_computation | async-start | bytes 98304 | tf_op jit(solution)/shard_map/all_to_all | solution.py:176
  477.1 41.1 %all-to-all-start.1 = ((bf16[4,2,196608]{2,1,0:T(2,128)(2,1)}), bf16[4,2,196608]{2,1,0:T(2,128)(2,1)S(1)}, u32[]{:S(2)}, u32[]{:S(2)}) async-start(bf16[4,2,196608]{2,1,0:T(2,128)(2,1)} %reshape.1080), calls=%async_computation.1 | async-start | bytes 6291456 | tf_op jit(solution)/shard_map/all_to_all | solution.py:175
  494.3 42.0 %copy-start.15 = (f32[2048]{0:T(1024)}, f32[2048]{0:T(1024)S(1)}, u32[]{:S(2)}) copy-start(f32[2048]{0:T(1024)S(1)} %get-tuple-element.1868) | copy-start | bytes 24580
  494.3 42.0 %copy-start.17 = (f32[2048]{0:T(1024)}, f32[2048]{0:T(1024)S(1)}, u32[]{:S(2)}) copy-start(f32[2048]{0:T(1024)S(1)} %get-tuple-element.1869) | copy-start | bytes 24580
  987.0 40.6 %all-to-all-start.2 = ((bf16[4,2,196608]{2,1,0:T(2,128)(2,1)}), bf16[4,2,196608]{2,1,0:T(2,128)(2,1)S(1)}, u32[]{:S(2)}, u32[]{:S(2)}) async-start(bf16[4,2,196608]{2,1,0:T(2,128)(2,1)} %reshape.1082), calls=%async_computation.2 | async-start | bytes 6291456 | tf_op jit(solution)/shard_map/all_to_all | solution.py:211
  1015.4 50.5 %copy-start.21 = (f32[8,1,384]{2,1,0:T(1,128)}, f32[8,1,384]{2,1,0:T(1,128)S(1)}, u32[]{:S(2)}) copy-start(f32[8,1,384]{2,1,0:T(1,128)S(1)} %convert_element_type.323) | copy-start | bytes 36868
  1045.4 20.6 slice-start
  1053.1 12.9 copy-start.37
  1053.1 12.9 copy-start
  1053.1 12.9 slice-start.1
  1124.7 40.6 %all-to-all-start.3 = ((bf16[4,2,196608]{2,1,0:T(2,128)(2,1)}), bf16[4,2,196608]{2,1,0:T(2,128)(2,1)S(1)}, u32[]{:S(2)}, u32[]{:S(2)}) async-start(bf16[4,2,196608]{2,1,0:T(2,128)(2,1)} %reshape.1084), calls=%async_computation.3 | async-start | bytes 6291456 | tf_op jit(solution)/shard_map/all_to_all | solution.py:225
  1128.4 869.1 %reduce-scatter.4.cloned.1.call-start = ((), (), s32[]{:S(2)}) async-start(), calls=%async_computation.11 | async-start | bytes 1310720 | tf_op jit(solution)/shard_map/reduce_scatter | solution.py:244
  1778.3 340.5 %reduce-scatter.8.cloned.1.call-start = ((), (), s32[]{:S(2)}) async-start(), calls=%async_computation.13 | async-start | bytes 21233664 | tf_op jit(solution)/shard_map/reduce_scatter | solution.py:268
  1806.6 24.7 copy-start.36
  1828.0 114.7 %all-to-all-start.5 = ((bf16[4,2,3072]{2,1,0:T(2,128)(2,1)}), bf16[4,2,3072]{2,1,0:T(2,128)(2,1)S(1)}, u32[]{:S(2)}, u32[]{:S(2)}) async-start(bf16[4,2,3072]{2,1,0:T(2,128)(2,1)} %reshape.1086), calls=%async_computation.6 | async-start | bytes 98304 | tf_op jit(solution)/shard_map/all_to_all | solution.py:242
  1831.3 20.7 copy-start.28
  1831.3 20.7 copy-start.30
  1831.3 20.7 copy-start.32
  1831.3 20.7 copy-start.34
  1942.7 40.7 %all-to-all-start.4 = ((bf16[4,2,196608]{2,1,0:T(2,128)(2,1)}), bf16[4,2,196608]{2,1,0:T(2,128)(2,1)S(1)}, u32[]{:S(2)}, u32[]{:S(2)}) async-start(bf16[4,2,196608]{2,1,0:T(2,128)(2,1)} %reshape.1088), calls=%async_computation.4 | async-start | bytes 6291456 | tf_op jit(solution)/shard_map/all_to_all | solution.py:241
  1946.4 815.7 %reduce-scatter.6.cloned.1.call-start = ((), (), s32[]{:S(2)}) async-start(), calls=%async_computation.12 | async-start | bytes 45121536 | tf_op jit(solution)/shard_map/reduce_scatter | solution.py:266
  2018.4 833.6 %all-reduce.36.cloned.1.call-start = ((), (), s32[]{:S(2)}) async-start(), calls=%async_computation.16 | async-start | bytes 7372800 | tf_op jit(solution)/shard_map/psum | solution.py:272
  2766.3 12.8 copy-start.59
  2766.3 13.8 copy-start.60
  2766.3 208.8 %all-reduce.34.cloned.1.call-start = ((), (), s32[]{:S(2)}) async-start(), calls=%async_computation.15 | async-start | bytes 142336 | tf_op jit(solution)/shard_map/psum | solution.py:235
  2780.1 26.7 copy-start.43
  2780.1 26.7 copy-start.9
  (60 other events, 387.6 us)
Sparse Core Ops, SparseCore 0:
  9.5 386.0 all-gather.5
  416.6 17.2 all-gather.9
  436.2 135.7 all-gather.7
  1778.4 23.9 reduce-scatter.3
  1806.7 312.0 reduce-scatter.7
  2123.1 639.0 reduce-scatter.5
  2766.4 78.1 all-reduce.35
  2852.0 123.0 all-reduce.33
where the time goes:
time: 3010 us; the launch traced here: 2990 us
  waiting for transfers between devices  1280 us (43%)
  local copies, waits for them, and re-layouts  850 us (28%)
  other arithmetic  352 us (12%)
  matrix products  335 us (11%)
  blocking collectives  107 us (4%)
    reduce_scatter x1, waiting for transfers between devices, shards(): lax.psum_scatter(in_weight_term, 'wshard', scatter_dimension=0, tiled=True)  641 us
    all_gather x1, waiting for transfers between devices, shards(): lax.all_gather(in_weight, 'wshard', axis=0, tiled=True)  339 us
    dynamic_update_slice x48, local copies, waits for them, and re-layouts, state_scan(): _, results = lax.scan(jax.checkpoint(block_step), start_state, pieces)  322 us
    dot_general x24, matrix products, block_step(): within = jnp.einsum('ijh,jhp->ihp', weighted, x_block, precision=precise)  124 us
    unnamed x10, other arithmetic  117 us
    psum x1, waiting for transfers between devices, shards(): lax.psum((kernel_sum, offset_sum, bias_sum, log_sum, skip_sum), ('wshard'...  117 us
    reduce_scatter x1, waiting for transfers between devices, shards(): lax.psum_scatter(out_weight_term, 'wshard', scatter_dimension=0, tiled=True)  99 us
    unnamed x157, local copies, waits for them, and re-layouts  93.5 us
  transfers between devices with their start and end apart: 14, of which 8 were waited for; matrix products, arithmetic and copies ran while one was open for 28% of the time, Pallas kernels for 0%

commit v1 on v0

--- a/solution.py
+++ b/solution.py
@@ -233,7 +233,7 @@
         mixer_pull(d_mixed_heads.astype(jnp.float32))
     )
     conv_weight_grad, conv_bias_grad, step_bias_grad, decay_log_grad, skip_scale_grad = lax.psum(
-        (kernel_sum, offset_sum, bias_sum, log_sum, skip_sum), ("wshard", "seq")
+        lax.psum((kernel_sum, offset_sum, bias_sum, log_sum, skip_sum), "seq"), "wshard"
     )
     d_x_low = d_x_heads.astype(jnp.bfloat16)
     d_dt_low = d_dt_heads.astype(jnp.bfloat16)

time: 3010 us -> 2920 us (0.970)
  waiting for transfers between devices: 1280 us -> 1190 us
    psum x1, waiting for transfers between devices: 117 us -> 6.71 us  [shards(): lax.psum((kernel_sum, offset_sum, bias_sum, log_sum, skip_sum), 'seq')]
    psum x1, waiting for transfers between devices: 0.01 us -> 34 us  [shards(): lax.psum(shard_sums[0].astype(jnp.bfloat16), 'seq').astype(jnp.float32)]
    unnamed x157 -> x150, local copies, waits for them, and re-layouts: 93.5 us -> 87.3 us
  transfers between devices with their start and end apart: 14 -> 14, of which waited for: 8 -> 9; matrix products, arithmetic and copies ran while one was open for 28% -> 29% of each run, Pallas kernels for 0% -> 0%
where the time goes in v1:
time: 2920 us; the launch traced here: 2890 us
  waiting for transfers between devices  1190 us (41%)
  local copies, waits for them, and re-layouts  844 us (29%)
  other arithmetic  352 us (12%)
  matrix products  332 us (11%)
  blocking collectives  111 us (4%)
    reduce_scatter x1, waiting for transfers between devices, shards(): lax.psum_scatter(in_weight_term, 'wshard', scatter_dimension=0, tiled=True)  641 us
    all_gather x1, waiting for transfers between devices, shards(): lax.all_gather(in_weight, 'wshard', axis=0, tiled=True)  339 us
    dynamic_update_slice x48, local copies, waits for them, and re-layouts, state_scan(): _, results = lax.scan(jax.checkpoint(block_step), start_state, pieces)  322 us
    dot_general x24, matrix products, block_step(): within = jnp.einsum('ijh,jhp->ihp', weighted, x_block, precision=precise)  124 us
    unnamed x10, other arithmetic  117 us
    unnamed x150, local copies, waits for them, and re-layouts  87.3 us
    reduce_scatter x1, waiting for transfers between devices, shards(): lax.psum_scatter(out_weight_term, 'wshard', scatter_dimension=0, tiled=True)  84.9 us
    unnamed x2, blocking collectives  79.6 us
  transfers between devices with their start and end apart: 14, of which 9 were waited for; matrix products, arithmetic and copies ran while one was open for 29% of the time, Pallas kernels for 0%

profile of v1, /device:TPU:8, one launch (start us, length us, event | category | flops | bytes accessed | tf_op | source)
XLA Modules:
  0.0 2892.3 jit_solution(561585640467802345)
XLA Ops:
  10.8 43.2 %all-reduce.24 = bf16[1536]{0:T(1024)(128)(2,1)S(1)} all-reduce(bf16[1536]{0:T(1024)(128)(2,1)S(1)} %dynamic-update-slice.15), channel_id=1, replica_groups=mesh['wshard'=8,'seq'=4] {'wshard'}, use_global_device_ids=true, to_apply=%add.24 | all-reduce | flops 1536 | bytes 6144
  56.5 339.2 %all-gather.6.cloned.1.call-done = bf16[1536,6448]{1,0:T(8,128)(2,1)} async-done(((bf16[192,6448]{1,0:T(8,128)(2,1)}), bf16[1536,6448]{1,0:T(8,128)(2,1)}) %all-gather.6.cloned.1.call-update) | async-done | bytes 19808272 | tf_op jit(solution)/shard_map/all_gather | solution.py:158
  425.8 27.4 copy.490
  453.2 20.3 reduce.35
  575.2 312.3 %while.143 = (s32[]{:T(128)}, f32[12,128,64]{1,2,0:T(8,128)S(1)}, f32[8,256,12,64]{1,0,3,2:T(8,128)}, f32[8,12,128,64]{2,3,1,0:T(8,128)}, f32[8,256,12]{1,2,0:T(...) while((s32[]{:T(128)}, f32[12,128,64]{1,2,0:T(8,128)S(1)}, ...), condition=%wide.region_4.5_spmd.clone, body=%wide.region_1.4_spmd.clone.sunk | while | flops 1314042880 | bytes 11014881 | solution.py:72
  592.4 18.5 dynamic_update_slice.219
  631.4 18.5 dynamic_update_slice.219
  670.4 18.5 dynamic_update_slice.219
  709.4 18.5 dynamic_update_slice.219
  748.4 18.5 dynamic_update_slice.219
  787.5 18.5 dynamic_update_slice.219
  826.5 18.5 dynamic_update_slice.219
  865.5 18.5 dynamic_update_slice.219
  908.2 44.7 %copy.489 = bf16[1,2048,768]{2,0,1:T(2,128)(2,1)} copy(bf16[1,2048,768]{2,1,0:T(8,128)(2,1)S(1)} %fusion.107) | data formatting | bytes 6291456 | tf_op jit(solution)/shard_map/convert_element_type | solution.py:212
  952.9 31.6 %reduce.36 = bf16[2048,768]{1,0:T(8,128)(2,1)S(1)} reduce(bf16[2048,1,768]{2,1,0:T(2,128)(2,1)} %bitcast.482, bf16[]{:T(256)} %broadcast.726), dimensions={1}, to_apply=%bitcast.320.reduce_sub_computation | reduce | bytes 6291458
  990.7 24.7 all-gather.1
  1073.3 27.4 copy.488
  1100.7 20.4 reduce.37
  1128.4 36.8 %all-to-all-done.3 = bf16[4,2,196608]{2,1,0:T(2,128)(2,1)S(1)} async-done(((bf16[4,2,196608]{2,1,0:T(2,128)(2,1)}), bf16[4,2,196608]{2,1,0:T(2,128)(2,1)S(1)}, u32[]{:S(2)}, u32[]{:S(2)}) %all-to-all-start.3) | async-done | bytes 3145760 | tf_op jit(solution)/shard_map/all_to_all | solution.py:225
  1198.6 566.3 %while.144 = (s32[]{:T(128)}, f32[12,128,64]{1,2,0:T(8,128)S(1)}, f32[8,256,12,64]{1,0,3,2:T(8,128)}, f32[8,256,128]{2,1,0:T(8,128)}, f32[8,256,128]{2,1,0:T(8,1...) while((s32[]{:T(128)}, f32[12,128,64]{1,2,0:T(8,128)S(1)}, ...), condition=%wide.region_19.20_spmd.clone, body=%wide.region_7.19_spmd.clone.sunk | while | flops 3038930944 | bytes 28993192 | solution.py:72
  1245.8 18.5 dynamic_update_slice.223
  1599.3 18.5 dynamic_update_slice.223
  1831.3 20.7 multiply_reduce_fusion.7
  1863.9 44.8 %copy.487 = bf16[1,2048,768]{2,0,1:T(2,128)(2,1)} copy(bf16[1,2048,768]{2,1,0:T(8,128)(2,1)S(1)} %fusion.111) | data formatting | bytes 6291456 | tf_op jit(solution)/shard_map/convert_element_type | solution.py:238
  1908.6 31.6 %reduce.39 = bf16[2048,768]{1,0:T(8,128)(2,1)S(1)} reduce(bf16[2048,1,768]{2,1,0:T(2,128)(2,1)} %bitcast.476, bf16[]{:T(256)} %broadcast.726), dimensions={1}, to_apply=%bitcast.318.reduce_sub_computation | reduce | bytes 6291458
  1951.7 31.7 %all-to-all-done.4 = bf16[4,2,196608]{2,1,0:T(2,128)(2,1)S(1)} async-done(((bf16[4,2,196608]{2,1,0:T(2,128)(2,1)}), bf16[4,2,196608]{2,1,0:T(2,128)(2,1)S(1)}, u32[]{:S(2)}, u32[]{:S(2)}) %all-to-all-start.4) | async-done | bytes 3145760 | tf_op jit(solution)/shard_map/all_to_all | solution.py:241
  1997.5 20.9 fusion.120
  2033.9 84.9 %reduce-scatter.8.cloned.1.call-done = f32[384,1536]{1,0:T(8,128)} async-done(((f32[3072,1536]{1,0:T(8,128)}), f32[384,1536]{1,0:T(8,128)}) %reduce-scatter.8.cloned.1.call-update) | async-done | bytes 2359312 | tf_op jit(solution)/shard_map/reduce_scatter | solution.py:268
  2121.6 640.6 %reduce-scatter.6.cloned.1.call-done = f32[192,6448]{1,0:T(8,128)} async-done(((f32[1536,6448]{1,0:T(8,128)}), f32[192,6448]{1,0:T(8,128)}) %reduce-scatter.6.cloned.1.call-update) | async-done | bytes 4952080 | tf_op jit(solution)/shard_map/reduce_scatter | solution.py:266
  2766.3 23.7 fusion.104
  2796.7 36.4 %all-reduce.38 = (bf16[1536]{0:T(1024)(128)(2,1)S(1)}, f32[4,3328]{1,0:T(4,128)}, f32[3328]{0:T(1024)}, f32[48]{0:T(128)}, f32[48]{0:T(128)}, /*index=5*/f32[48]{0:T(128)}, bf16[3072]{0:T(1024)(128)(2,1)S(1)}) all-reduce(f32[1536]{0:T(1024)S(1)} %get-tuple-element.1746, ...), channel_id=4, replica_groups=mesh['wshard'=8,'seq'=4] {'wshard'}, use_global_device_ids=true, to_apply=%region_23.24.clone | all-reduce | flops 21392 | bytes 161920
  2845.2 34.0 %all-reduce.37.cloned.1.call-done = (bf16[192,6448]{1,0:T(8,128)(2,1)}, bf16[384,1536]{1,0:T(8,128)(2,1)}) async-done(((bf16[192,6448]{1,0:T(8,128)(2,1)}, bf16[384,1536]{1,0:T(8,128)(2,1)}), (bf16[192,6448]{1,0:T(8,128)(2,1)}, bf16[384,1536]{1,0:T(8,128)(2,1)})) %all-reduce.37.cloned.1.call-update) | async-done | bytes 3655696 | tf_op jit(solution)/shard_map/psum | solution.py:272
  (1033 shorter events, 1081.5 us)
Async XLA Ops:
  7.2 388.5 %all-gather.6.cloned.1.call-start = ((), (), s32[]{:S(2)}) async-start(), calls=%async_computation.9 | async-start | bytes 22560768 | tf_op jit(solution)/shard_map/all_gather | solution.py:158
  7.9 494.1 %all-gather.10.cloned.1.call-start = ((), (), s32[]{:S(2)}) async-start(), calls=%async_computation.14 | async-start | bytes 1310720 | tf_op jit(solution)/shard_map/all_gather | solution.py:178
  54.0 359.0 %copy-start.39 = (f32[1536]{0:T(1024)}, f32[1536]{0:T(1024)S(1)}, u32[]{:S(2)}) copy-start(f32[1536]{0:T(1024)S(1)} %convert_element_type.262) | copy-start | bytes 18436
  56.5 356.6 %copy-start.50 = (f32[512]{0:T(512)}, f32[512]{0:T(512)S(1)}, u32[]{:S(2)}) copy-start(f32[512]{0:T(512)S(1)} %fusion.144) | copy-start | bytes 6148
  416.5 636.6 %all-gather.8.cloned.1.call-start = ((), (), s32[]{:S(2)}) async-start(), calls=%async_computation.10 | async-start | bytes 10616832 | tf_op jit(solution)/shard_map/all_gather | solution.py:160
  420.2 56.9 %all-to-all-start = ((bf16[4,2,3072]{2,1,0:T(2,128)(2,1)}), bf16[4,2,3072]{2,1,0:T(2,128)(2,1)S(1)}, u32[]{:S(2)}, u32[]{:S(2)}) async-start(bf16[4,2,3072]{2,1,0:T(2,128)(2,1)} %reshape.1078), calls=%async_computation | async-start | bytes 98304 | tf_op jit(solution)/shard_map/all_to_all | solution.py:176
  473.6 12.0 copy-start.41
  477.1 41.1 %all-to-all-start.1 = ((bf16[4,2,196608]{2,1,0:T(2,128)(2,1)}), bf16[4,2,196608]{2,1,0:T(2,128)(2,1)S(1)}, u32[]{:S(2)}, u32[]{:S(2)}) async-start(bf16[4,2,196608]{2,1,0:T(2,128)(2,1)} %reshape.1080), calls=%async_computation.1 | async-start | bytes 6291456 | tf_op jit(solution)/shard_map/all_to_all | solution.py:175
  494.3 42.0 %copy-start.15 = (f32[2048]{0:T(1024)}, f32[2048]{0:T(1024)S(1)}, u32[]{:S(2)}) copy-start(f32[2048]{0:T(1024)S(1)} %get-tuple-element.1873) | copy-start | bytes 24580
  494.3 42.0 %copy-start.17 = (f32[2048]{0:T(1024)}, f32[2048]{0:T(1024)S(1)}, u32[]{:S(2)}) copy-start(f32[2048]{0:T(1024)S(1)} %get-tuple-element.1874) | copy-start | bytes 24580
  987.0 40.6 %all-to-all-start.2 = ((bf16[4,2,196608]{2,1,0:T(2,128)(2,1)}), bf16[4,2,196608]{2,1,0:T(2,128)(2,1)S(1)}, u32[]{:S(2)}, u32[]{:S(2)}) async-start(bf16[4,2,196608]{2,1,0:T(2,128)(2,1)} %reshape.1082), calls=%async_computation.2 | async-start | bytes 6291456 | tf_op jit(solution)/shard_map/all_to_all | solution.py:211
  1015.4 50.5 %copy-start.21 = (f32[8,1,384]{2,1,0:T(1,128)}, f32[8,1,384]{2,1,0:T(1,128)S(1)}, u32[]{:S(2)}) copy-start(f32[8,1,384]{2,1,0:T(1,128)S(1)} %convert_element_type.323) | copy-start | bytes 36868
  1045.4 20.6 slice-start
  1053.1 12.9 copy-start.37
  1053.1 12.9 copy-start
  1053.1 12.9 slice-start.1
  1124.7 40.6 %all-to-all-start.3 = ((bf16[4,2,196608]{2,1,0:T(2,128)(2,1)}), bf16[4,2,196608]{2,1,0:T(2,128)(2,1)S(1)}, u32[]{:S(2)}, u32[]{:S(2)}) async-start(bf16[4,2,196608]{2,1,0:T(2,128)(2,1)} %reshape.1084), calls=%async_computation.3 | async-start | bytes 6291456 | tf_op jit(solution)/shard_map/all_to_all | solution.py:225
  1128.4 869.1 %reduce-scatter.4.cloned.1.call-start = ((), (), s32[]{:S(2)}) async-start(), calls=%async_computation.11 | async-start | bytes 1310720 | tf_op jit(solution)/shard_map/reduce_scatter | solution.py:244
  1778.3 340.5 %reduce-scatter.8.cloned.1.call-start = ((), (), s32[]{:S(2)}) async-start(), calls=%async_computation.13 | async-start | bytes 21233664 | tf_op jit(solution)/shard_map/reduce_scatter | solution.py:268
  1806.6 24.7 copy-start.36
  1828.0 114.7 %all-to-all-start.5 = ((bf16[4,2,3072]{2,1,0:T(2,128)(2,1)}), bf16[4,2,3072]{2,1,0:T(2,128)(2,1)S(1)}, u32[]{:S(2)}, u32[]{:S(2)}) async-start(bf16[4,2,3072]{2,1,0:T(2,128)(2,1)} %reshape.1086), calls=%async_computation.6 | async-start | bytes 98304 | tf_op jit(solution)/shard_map/all_to_all | solution.py:242
  1831.3 20.7 copy-start.28
  1831.3 20.7 copy-start.30
  1831.3 20.7 copy-start.32
  1831.3 20.7 copy-start.34
  1942.7 40.7 %all-to-all-start.4 = ((bf16[4,2,196608]{2,1,0:T(2,128)(2,1)}), bf16[4,2,196608]{2,1,0:T(2,128)(2,1)S(1)}, u32[]{:S(2)}, u32[]{:S(2)}) async-start(bf16[4,2,196608]{2,1,0:T(2,128)(2,1)} %reshape.1088), calls=%async_computation.4 | async-start | bytes 6291456 | tf_op jit(solution)/shard_map/all_to_all | solution.py:241
  1946.4 815.7 %reduce-scatter.6.cloned.1.call-start = ((), (), s32[]{:S(2)}) async-start(), calls=%async_computation.12 | async-start | bytes 45121536 | tf_op jit(solution)/shard_map/reduce_scatter | solution.py:266
  2018.5 778.2 %all-reduce.35.cloned.1.call-start = ((), (), s32[]{:S(2)}) async-start(), calls=%async_computation.15 | async-start | bytes 142336 | tf_op jit(solution)/shard_map/psum | solution.py:236
  2022.3 856.8 %all-reduce.37.cloned.1.call-start = ((), (), s32[]{:S(2)}) async-start(), calls=%async_computation.16 | async-start | bytes 7372800 | tf_op jit(solution)/shard_map/psum | solution.py:272
  2766.3 30.4 %copy-start.45 = (f32[3072]{0:T(1024)S(1)}, f32[3072]{0:T(1024)}, u32[]{:S(2)}) copy-start(f32[3072]{0:T(1024)} %get-tuple-element.1739) | copy-start | bytes 36868
  2766.3 74.4 %copy-start.43 = (f32[512]{0:T(512)S(1)}, f32[512]{0:T(512)}, u32[]{:S(2)}) copy-start(f32[512]{0:T(512)} %copy-done.42) | copy-start | bytes 6148
  2766.3 74.4 %copy-start.9 = (bf16[1,512,1536]{2,1,0:T(8,128)(2,1)S(1)}, bf16[1,512,1536]{2,1,0:T(8,128)(2,1)}, u32[]{:S(2)}) copy-start(bf16[1,512,1536]{2,1,0:T(8,128)(2,1)} %param.27) | copy-start | bytes 4718596
  (59 other events, 354.1 us)
Sparse Core Ops, SparseCore 0:
  9.5 386.0 all-gather.5
  416.6 17.2 all-gather.9
  436.2 135.7 all-gather.7
  1778.4 23.9 reduce-scatter.3
  1806.7 312.0 reduce-scatter.7
  2123.1 639.0 reduce-scatter.5
  2765.9 30.7 all-reduce.34
  2799.8 79.2 all-reduce.36
